TPU v7x, 32 devices: a whole 2x2x4 slice. The times are simulated.
32 devices in a mesh: wide: 4 (over z), narrow: 8 (over y, x, core).
Axes of the slice: x: 2, y: 2, z: 4, core: 2. Of those that a mesh axis runs over, the one named last changes fastest.
Arguments:
- kernel: bfloat16 [2048, 2048], P('wide', 'narrow'), may hold values from -0.15625 to 0.15625
- hamiltonian: bfloat16 [2048, 2048], P('wide', 'narrow'), may hold values from -6 to 6
- kernel_tiles: int32 [32, 32], P('wide', 'narrow'), may hold values from 0 to 1, as said below
- ham_tiles: int32 [32, 32], P('wide', 'narrow'), may hold values from 0 to 1, as said below
- pair_row: int32 [2048], P(('wide', 'narrow')), may hold values from 0 to 7
- pair_col: int32 [2048], P(('wide', 'narrow')), may hold values from 0 to 3
- sphere_phi: bfloat16 [2048, 64, 512], P(('wide', 'narrow')), may hold values from -0.09375 to 0.09375
- owner: int32 [8, 4], P('narrow'), may hold values from 0 to 3, each once within a row
Outputs:
- gradient: float32 [32, 64, 512], P(('wide', 'narrow'))
Inputs may be any that keep to these rules, and one draw needn't show every extreme that they name: Each row of owner is a permutation of 0 to 3. `kernel_tiles`: in each tile row, at most 4 ones fall among one narrow index's 4 tile columns, and some row has that many. `ham_tiles`: in each tile column, at most 7 ones fall among one wide index's 8 tile rows, and some column has that many.
All inputs are finite; a program needn't handle non-finite values.
Results may differ from a plain program's by a relative error of at most 0.0029.
Values may be sent and summed in bfloat16 or wider, within the bound.
A program may use at most 128 MiB of HBM per device.

v0:
```python
import jax
import jax.numpy as jnp
from jax import lax
from jax.sharding import PartitionSpec as P


def expand(mask_tiles, tile_width):
    return jnp.repeat(jnp.repeat(mask_tiles, tile_width, axis=0), tile_width, axis=1)


def collect_kernel(kmasked):
    gathered = lax.all_gather(kmasked, "narrow", axis=1, tiled=True)
    return gathered


def body(kernel, hamiltonian, kernel_tiles, ham_tiles, pair_row, pair_col, sphere_phi, owner):
    tile_width = sphere_phi.shape[1]
    kmasked = kernel * expand(kernel_tiles, tile_width).astype(jnp.bfloat16)
    hmasked = hamiltonian * expand(ham_tiles, tile_width).astype(jnp.bfloat16)
    height = kernel.shape[0]
    breadth = hamiltonian.shape[1]
    kernel_full = collect_kernel(kmasked)
    coefficients = jnp.dot(
        kernel_full,
        lax.all_gather(hmasked, "wide", axis=0, tiled=True),
        preferred_element_type=jnp.float32,
    )
    coefficients = coefficients.astype(jnp.bfloat16)
    tile_rows = height // tile_width
    tile_cols = breadth // tile_width
    tile_table = coefficients.reshape(tile_rows, tile_width, tile_cols, tile_width).transpose(
        0, 2, 1, 3
    )
    tile_blocks = tile_table[pair_row, pair_col]
    gradient_blocks = jnp.einsum(
        "pij,pir->pjr", tile_blocks, sphere_phi, preferred_element_type=jnp.float32
    )
    local_owner = owner[0]
    column_ids = jnp.arange(tile_cols, dtype=jnp.int32)
    dest_slot = jnp.sum(
        jnp.where(pair_col[:, None] == column_ids[None, :], local_owner[None, :], 0), axis=1
    )
    chooser = (dest_slot[None, :] == column_ids[:, None]).astype(jnp.float32)
    partials = jnp.einsum("qp,pjr->qjr", chooser, gradient_blocks, precision=lax.Precision.HIGHEST)
    return lax.psum_scatter(partials, "wide", scatter_dimension=0, tiled=True)


def solution(mesh):
    return jax.shard_map(
        body,
        mesh=mesh,
        in_specs=(
            P("wide", "narrow"),
            P("wide", "narrow"),
            P("wide", "narrow"),
            P("wide", "narrow"),
            P(("wide", "narrow")),
            P(("wide", "narrow")),
            P(("wide", "narrow"), None, None),
            P("narrow", None),
        ),
        out_specs=P(("wide", "narrow"), None, None),
        check_vma=False,
    )
```

profile of v0, /device:TPU:0, one launch (start us, length us, event | category | flops | bytes accessed | tf_op | source)
XLA Modules:
  0.0 113.4 jit_solution(17894622116828058528)
XLA Ops:
  6.5 1.1 copy.23
  7.6 0.7 convert_element_type.29
  8.3 0.1 broadcast_in_dim.41
  8.4 0.1 convert_element_type.30
  8.5 0.7 bitcast_multiply_fusion
  9.2 0.0 all-gather.3.cloned.1.call-start
  9.3 1.1 copy.22
  10.4 0.7 convert_element_type.26
  11.1 0.1 broadcast_in_dim.39
  11.1 0.1 convert_element_type.27
  11.2 0.7 bitcast_multiply_fusion.1
  12.0 0.0 reduce-scatter.2.cloned.1.call-start
  12.0 0.8 select_reduce_fusion
  12.8 0.7 fusion.7
  13.5 26.6 %all-gather.5.cloned.1.call-done = bf16[2048,256]{0,1:T(8,128)(2,1)} async-done(((bf16[512,256]{0,1:T(8,128)(2,1)}), bf16[2048,256]{0,1:T(8,128)(2,1)}) %all-gather.5.cloned.1.call-update) | async-done | bytes 1048592 | tf_op jit(solution)/shard_map/all_gather | solution.py:25
  40.1 29.1 %all-gather.3.cloned.1.call-done = bf16[512,2048]{0,1:T(8,128)(2,1)} async-done(((bf16[512,256]{0,1:T(8,128)(2,1)}), bf16[512,2048]{0,1:T(8,128)(2,1)}) %all-gather.3.cloned.1.call-update) | async-done | bytes 2097168 | tf_op jit(solution)/shard_map/all_gather | solution.py:12
  69.2 2.6 %convolution_convert_fusion = bf16[512,256]{1,0:T(8,128)(2,1)S(1)} fusion(bf16[512,2048]{0,1:T(8,128)(2,1)} %all-gather.3.cloned.1.call-done, bf16[2048,256]{0,1:T(8,128)(2,1)} %all-gather.5.cloned.1.call-done), kind=kOutput, calls=%fused_computation.3 | convolution fusion | flops 537001984 | bytes 3407872 | tf_op jit(solution)/shard_map/dot_general | solution.py:23
  71.8 0.2 reshape.13
  72.0 0.1 copy.32
  72.2 0.8 gather_fusion
  73.0 3.5 %fusion.10 = f32[64,64,512]{2,1,0:T(8,128)S(1)} fusion(bf16[64,64,64]{2,1,0:T(8,128)(2,1)S(1)} %gather_fusion, bf16[64,64,512]{2,1,0:T(8,128)(2,1)} %param.14), kind=kOutput, calls=%fused_computation.19 | convolution fusion | flops 268435456 | bytes 13107200 | tf_op jit(solution)/shard_map/pij,pir->pjr/dot_general | solution.py:35
  76.5 7.5 %fusion = f32[4,64,512]{2,0,1:T(4,128)S(1)} fusion(f32[64,64,512]{2,1,0:T(8,128)S(1)} %fusion.10, s32[64]{0:T(128)S(1)} %select_reduce_fusion), kind=kOutput, calls=%fused_computation.1 | convolution fusion | flops 100663552 | bytes 8913152 | tf_op jit(solution)/shard_map/qp,pjr->qjr/dot_general | solution.py:44
  83.9 1.0 copy.27
  84.9 22.0 %reduce-scatter.2.cloned.1.call-done = f32[1,64,512]{2,1,0:T(8,128)} async-done(((f32[4,64,512]{2,1,0:T(8,128)}), f32[1,64,512]{2,1,0:T(8,128)}) %reduce-scatter.2.cloned.1.call-update) | async-done | bytes 131088 | tf_op jit(solution)/shard_map/reduce_scatter | solution.py:45
  (4 shorter events, 0.1 us)
Async XLA Ops:
  6.5 33.6 %all-gather.5.cloned.1.call-start = ((), (), s32[]{:S(2)}) async-start(), calls=%async_computation.2 | async-start | bytes 1310720 | tf_op jit(solution)/shard_map/all_gather | solution.py:25
  9.2 59.9 %all-gather.3.cloned.1.call-start = ((), (), s32[]{:S(2)}) async-start(), calls=%async_computation.1 | async-start | bytes 2359296 | tf_op jit(solution)/shard_map/all_gather | solution.py:12
  12.0 94.9 %reduce-scatter.2.cloned.1.call-start = ((), (), s32[]{:S(2)}) async-start(), calls=%async_computation.3 | async-start | bytes 655360 | tf_op jit(solution)/shard_map/reduce_scatter | solution.py:45
Sparse Core Ops, SparseCore 0:
  9.3 30.6 all-gather.4
  42.0 27.1 all-gather.2
  85.0 21.8 reduce-scatter.1
where the time goes:
time: 114 us; the launch traced here: 113 us
  waiting for transfers between devices  77.7 us (68%)
  matrix products  13.6 us (12%)
  between operations  13.2 us (12%)
  local copies, waits for them, and re-layouts  4.63 us (4%)
  other arithmetic  4.25 us (4%)
    all_gather x1, waiting for transfers between devices, collect_kernel(): gathered = lax.all_gather(kmasked, 'narrow', axis=1, tiled=True)  29.1 us
    all_gather x1, waiting for transfers between devices, body(): lax.all_gather(hmasked, 'wide', axis=0, tiled=True)  26.6 us
    reduce_scatter x1, waiting for transfers between devices, body(): return lax.psum_scatter(partials, 'wide', scatter_dimension=0, tiled=True)  22 us
    dot_general x1, matrix products, body(): jnp.einsum('qp,pjr->qjr', chooser, gradient_blocks, precision=lax.Precisi...  7.47 us
    dot_general x1, matrix products, body(): jnp.einsum('pij,pir->pjr', tile_blocks, sphere_phi, preferred_element_typ...  3.48 us
    dot_general x1, matrix products, body(): jnp.dot(kernel_full, lax.all_gather(hmasked, 'wide', axis=0, tiled=True),...  2.61 us
  transfers between devices with their start and end apart: 3, of which 3 were waited for; matrix products, arithmetic and copies ran while one was open for 4% of the time, Pallas kernels for 0%

commit v1 on v0

v1 whole, which is shorter than its diff:
```python
import functools

import jax
import jax.numpy as jnp
from jax import lax
from jax.experimental import pallas as pl
from jax.experimental.pallas import tpu as pltpu
from jax.sharding import PartitionSpec as P

MESH = pl.DeviceIdType.MESH
CHUNKS = 2
NT = (((1,), (1,)), ((), ()))


def xor(a, b, size):
    total, bit = 0, 1
    while bit < size:
        total = total + ((a // bit + b // bit) % 2) * bit
        bit *= 2
    return total


def kernel_body(
    n_wide, n_narrow, tile,
    ktiles, htiles, rows, cols, owner, k_hbm, h_hbm, phi_hbm, out_ref,
    k_in, h_in, phi, kbuf, hbuf, acc, table, lhs, own, stage, landed,
    in_sem, k_send, k_recv, s_send, s_recv, h_send, h_recv, r_send, r_recv,
):
    z = lax.axis_index("wide")
    n = lax.axis_index("narrow")
    chips = n_narrow // 2
    chip, core = n // 2, n % 2
    tile_rows, tile_cols = htiles.shape
    height, kcols = k_hbm.shape
    hrows, breadth = h_hbm.shape
    per = hrows // kcols
    width = breadth // CHUNKS
    jc = tile // CHUNKS
    pairs = rows.shape[0]
    half = width // 2

    barrier = pltpu.get_barrier_semaphore()

    def at(w, m):
        return (w, m)

    for g in range(1, chips):
        pl.semaphore_signal(barrier, inc=1, device_id=at(z, xor(chip, g, chips) * 2 + core), device_id_type=MESH)
    pl.semaphore_signal(barrier, inc=1, device_id=at(z, chip * 2 + 1 - core), device_id_type=MESH)
    for s in range(1, n_wide):
        pl.semaphore_signal(barrier, inc=1, device_id=at((z + s) % n_wide, n), device_id_type=MESH)

    load_h = pltpu.make_async_copy(h_hbm, h_in, in_sem.at[0])
    load_k = pltpu.make_async_copy(k_hbm, k_in, in_sem.at[1])
    load_p = pltpu.make_async_copy(phi_hbm, phi, in_sem.at[2])
    load_h.start()
    load_k.start()
    load_p.start()

    def mask_rows(tiles, b, extent):
        lane_tile = lax.broadcasted_iota(jnp.int32, (1, extent), 1) // tile
        mask = jnp.zeros((1, extent), jnp.float32)
        for a in range(tile_cols):
            mask = jnp.where(lane_tile == a, tiles[b, a].astype(jnp.float32), mask)
        return mask.astype(jnp.bfloat16)

    load_h.wait()
    for b in range(tile_rows):
        span = pl.ds(b * tile, tile)
        h_in[span, :] = h_in[span, :] * mask_rows(htiles, b, breadth)
    for c in range(CHUNKS):
        r = lax.broadcasted_iota(jnp.int32, (width, breadth), 0)
        col = lax.broadcasted_iota(jnp.int32, (width, breadth), 1)
        pick = (col == (r // jc) * tile + c * jc + r % jc).astype(jnp.float32).astype(jnp.bfloat16)
        hbuf[c, z] = lax.dot_general(pick, h_in[...], NT, preferred_element_type=jnp.float32).astype(jnp.bfloat16)
    load_k.wait()
    for b in range(tile_rows):
        span = pl.ds(b * tile, tile)
        kbuf[n, span, :] = k_in[span, :] * mask_rows(ktiles, b, kcols)

    pl.semaphore_wait(barrier, chips - 1 + 1 + n_wide - 1)

    def unit(u, src):
        if u == 0:
            return hbuf.at[0, src]
        return hbuf.at[1, src, pl.ds((u - 1) * half, half), :]

    def h_copy(u, way, s, src):
        ref = unit(u, src)
        return pltpu.make_async_remote_copy(
            src_ref=ref, dst_ref=ref, send_sem=h_send.at[u, way, s], recv_sem=h_recv.at[u, way, s],
            device_id=at(z + 1 if way == 0 else z - 1, n), device_id_type=MESH)

    def source(way, s):
        return z - s if way == 0 else z + s

    def has_next(way):
        return z < n_wide - 1 if way == 0 else z > 0

    def has_source(way, s):
        return z >= s if way == 0 else z < n_wide - s

    def h_start(u, way, s):
        h_copy(u, way, s, source(way, s)).start()

    def h_own(u):
        for way in range(2):
            @pl.when(has_next(way))
            def _():
                h_start(u, way, 0)

    def h_arrive(u, s):
        for way in range(2):
            @pl.when(has_source(way, s))
            def _():
                h_copy(u, way, s - 1, source(way, s)).wait_recv()
                if s < n_wide - 1:
                    @pl.when(has_next(way))
                    def _():
                        h_start(u, way, s)

    def slot(g, c):
        return kbuf.at[xor(chip, g, chips) * 2 + c]

    def k_copy(g):
        ref = slot(0, core)
        return pltpu.make_async_remote_copy(
            src_ref=ref, dst_ref=ref, send_sem=k_send.at[g], recv_sem=k_recv.at[g],
            device_id=at(z, xor(chip, g, chips) * 2 + core), device_id_type=MESH)

    def k_arrived(g):
        ref = slot(g, core)
        pltpu.make_async_remote_copy(
            src_ref=ref, dst_ref=ref, send_sem=k_send.at[g], recv_sem=k_recv.at[g],
            device_id=at(z, xor(chip, g, chips) * 2 + core), device_id_type=MESH).wait_recv()

    def sib_copy(g, c):
        ref = slot(g, c)
        return pltpu.make_async_remote_copy(
            src_ref=ref, dst_ref=ref, send_sem=s_send.at[g], recv_sem=s_recv.at[g],
            device_id=at(z, chip * 2 + 1 - core), device_id_type=MESH)

    h_own(0)
    h_own(1)
    for g in range(1, chips):
        k_copy(g).start()
    sib_copy(0, core).start()

    h_arrive(0, 1)
    h_own(2)
    for s in range(2, n_wide - 1):
        h_arrive(0, s)
    for g in range(1, chips - 1):
        k_arrived(g)
        sib_copy(g, core).start()
    h_arrive(1, 1)
    h_arrive(2, 1)
    k_arrived(chips - 1)
    sib_copy(chips - 1, core).start()
    h_arrive(0, n_wide - 1)
    for s in range(2, n_wide - 1):
        h_arrive(1, s)
        h_arrive(2, s)
    for g in range(chips):
        sib_copy(g, 1 - core).wait_recv()

    def accumulate(c, w):
        total = acc[...]
        for i in range(per):
            total = total + lax.dot_general(
                hbuf[c, w, :, i * kcols:(i + 1) * kcols], kbuf[w * per + i], NT,
                preferred_element_type=jnp.float32)
        acc[...] = total

    lane = lax.broadcasted_iota(jnp.int32, (1, 2 * tile), 1)
    low = lane < tile

    def finish(c):
        for b2 in range(tile_rows // 2):
            x = acc[:, 2 * tile * b2:2 * tile * (b2 + 1)].astype(jnp.bfloat16).astype(jnp.float32)
            y = pltpu.roll(x, tile, 1)
            for odd in range(2):
                both = jnp.where(low, x, y) if odd == 0 else jnp.where(low, y, x)
                for a in range(tile_cols):
                    table[(2 * b2 + odd) * tile_cols + a] = both[a * jc:(a + 1) * jc]

        def place(t, carry):
            c0, c1 = cols[2 * t], cols[2 * t + 1]
            first = table[rows[2 * t] * tile_cols + c0]
            second = table[rows[2 * t + 1] * tile_cols + c1]
            both = jnp.where(low, first, second)
            dest = jnp.where(low, owner[0, c0], owner[0, c1])
            at_lane = pl.ds(pl.multiple_of(t * 2 * tile, 2 * tile), 2 * tile)
            for d in range(n_wide):
                lhs[d * jc:(d + 1) * jc, at_lane] = jnp.where(dest == d, both, 0.0).astype(jnp.bfloat16)
            return carry

        lax.fori_loop(0, pairs // 2, place, 0, unroll=4)
        blocks = jnp.dot(lhs[...], phi[...], preferred_element_type=jnp.float32)
        for d in range(n_wide):
            piece = blocks[d * jc:(d + 1) * jc]
            own[c, d] = piece
            stage[c, d] = piece.astype(jnp.bfloat16)

    def r_copy(c, s):
        return pltpu.make_async_remote_copy(
            src_ref=stage.at[c, (z + s) % n_wide], dst_ref=landed.at[c, s - 1],
            send_sem=r_send.at[c, s - 1], recv_sem=r_recv.at[c, s - 1],
            device_id=at((z + s) % n_wide, n), device_id_type=MESH)

    def loop(c, lo, hi):
        acc[...] = jnp.zeros_like(acc)

        def step(w, carry):
            accumulate(c, w)
            return carry

        lax.fori_loop(lo, hi, step, 0)

    load_p.wait()
    loop(0, 0, n_wide)
    finish(0)
    for s in range(1, n_wide):
        r_copy(0, s).start()
    loop(1, z // (n_wide - 1), n_wide - (n_wide - 1 - z) // (n_wide - 1))
    h_arrive(1, n_wide - 1)
    h_arrive(2, n_wide - 1)

    @pl.when(z == 0)
    def _():
        accumulate(1, n_wide - 1)

    @pl.when(z == n_wide - 1)
    def _():
        accumulate(1, 0)

    finish(1)
    for s in range(1, n_wide):
        r_copy(1, s).start()

    for c in range(CHUNKS):
        total = own[c, z]
        for s in range(1, n_wide):
            r_copy(c, s).wait_recv()
            total = total + landed[c, s - 1].astype(jnp.float32)
        out_ref[0, c * jc:(c + 1) * jc, :] = total

    for c in range(CHUNKS):
        for s in range(1, n_wide):
            r_copy(c, s).wait_send()
    for g in range(1, chips):
        k_copy(g).wait_send()
    for g in range(chips):
        sib_copy(g, core).wait_send()
    for u in range(3):
        for way in range(2):
            for s in range(n_wide - 1):
                @pl.when(has_next(way) & has_source(way, s))
                def _():
                    h_copy(u, way, s, source(way, s)).wait_send()


def body(n_wide, n_narrow, kernel, hamiltonian, kernel_tiles, ham_tiles, pair_row, pair_col, sphere_phi, owner):
    pairs, tile, pts = sphere_phi.shape
    height, kcols = kernel.shape
    hrows, breadth = hamiltonian.shape
    tile_rows, tile_cols = ham_tiles.shape
    width, jc = breadth // CHUNKS, tile // CHUNKS
    chips = n_narrow // 2
    smem = pl.BlockSpec(memory_space=pltpu.SMEM)
    hbm = pl.BlockSpec(memory_space=pl.ANY)
    dma = pltpu.SemaphoreType.DMA
    return pl.pallas_call(
        functools.partial(kernel_body, n_wide, n_narrow, tile),
        out_shape=jax.ShapeDtypeStruct((1, tile, pts), jnp.float32),
        in_specs=[smem] * 5 + [hbm] * 3,
        out_specs=pl.BlockSpec(memory_space=pltpu.VMEM),
        scratch_shapes=[
            pltpu.VMEM((height, kcols), jnp.bfloat16),
            pltpu.VMEM((hrows, breadth), jnp.bfloat16),
            pltpu.VMEM((pairs * tile, pts), jnp.bfloat16),
            pltpu.VMEM((n_narrow, height, kcols), jnp.bfloat16),
            pltpu.VMEM((CHUNKS, n_wide, width, hrows), jnp.bfloat16),
            pltpu.VMEM((width, height), jnp.float32),
            pltpu.VMEM((tile_rows * tile_cols, jc, 2 * tile), jnp.float32),
            pltpu.VMEM((n_wide * jc, pairs * tile), jnp.bfloat16),
            pltpu.VMEM((CHUNKS, n_wide, jc, pts), jnp.float32),
            pltpu.VMEM((CHUNKS, n_wide, jc, pts), jnp.bfloat16),
            pltpu.VMEM((CHUNKS, n_wide - 1, jc, pts), jnp.bfloat16),
            dma((3,)),
            dma((chips,)), dma((chips,)),
            dma((chips,)), dma((chips,)),
            dma((3, 2, n_wide)), dma((3, 2, n_wide)),
            dma((CHUNKS, n_wide)), dma((CHUNKS, n_wide)),
        ],
        compiler_params=pltpu.CompilerParams(
            collective_id=0, has_side_effects=True, vmem_limit_bytes=60 * 2**20),
    )(kernel_tiles, ham_tiles, pair_row, pair_col, owner, kernel, hamiltonian,
      sphere_phi.reshape(pairs * tile, pts))


def solution(mesh):
    return jax.shard_map(
        functools.partial(body, mesh.shape["wide"], mesh.shape["narrow"]),
        mesh=mesh,
        in_specs=(
            P("wide", "narrow"),
            P("wide", "narrow"),
            P("wide", "narrow"),
            P("wide", "narrow"),
            P(("wide", "narrow")),
            P(("wide", "narrow")),
            P(("wide", "narrow"), None, None),
            P("narrow", None),
        ),
        out_specs=P(("wide", "narrow"), None, None),
        check_vma=False,
    )
```

time: 114 us -> 37.2 us (0.33)
  waiting for transfers between devices: 77.7 us -> 0 us
  Pallas kernels: 0 us -> 32.7 us
  matrix products: 13.6 us -> 0 us
  between operations: 13.2 us -> 0.01 us
  other arithmetic: 4.25 us -> 0 us
    all_gather x2 -> x0, waiting for transfers between devices: 55.7 us -> none  [the longest x1 29.1 us: collect_kernel(): gathered = lax.all_gather(kmasked, 'narrow', axis=1, tiled=True)]
    pallas_call x0 -> x1, Pallas kernels: none -> 32.7 us  [body(): pl.pallas_call(functools.partial(kernel_body, n_wide, n_narrow, tile), ou...]
    reduce_scatter x1 -> x0, waiting for transfers between devices: 22 us -> none  [body(): return lax.psum_scatter(partials, 'wide', scatter_dimension=0, tiled=True)]
    dot_general x3 -> x0, matrix products: 13.6 us -> none  [the longest x1 7.47 us: body(): jnp.einsum('qp,pjr->qjr', chooser, gradient_blocks, precision=lax.Precisi...]
    unnamed x2 -> x3, local copies, waits for them, and re-layouts: 2.18 us -> 4.26 us
    mul x2 -> x0, other arithmetic: 1.44 us -> none  [the longest x1 0.73 us: body(): kmasked = kernel * expand(kernel_tiles, tile_width).astype(jnp.bfloat16)]
    convert_element_type x2 -> x0, other arithmetic: 1.37 us -> none  [the longest x1 0.69 us: body(): hmasked = hamiltonian * expand(ham_tiles, tile_width).astype(jnp.bfloat16)]
  transfers between devices with their start and end apart: 3 -> 0, of which waited for: 3 -> 0; matrix products, arithmetic and copies ran while one was open for 4% -> 0% of each run, Pallas kernels for 0% -> 0%
where the time goes in v1:
time: 37.2 us; the launch traced here: 37 us
  Pallas kernels  32.7 us (88%)
  local copies, waits for them, and re-layouts  4.26 us (11%)
    pallas_call x1, Pallas kernels, body(): pl.pallas_call(functools.partial(kernel_body, n_wide, n_narrow, tile), ou...  32.7 us
    unnamed x3, local copies, waits for them, and re-layouts  4.26 us

profile of v1, /device:TPU:0, one launch (start us, length us, event | category | flops | bytes accessed | tf_op | source)
XLA Modules:
  0.0 37.0 jit_solution(14823812793480974542)
XLA Ops:
  0.0 1.3 %copy.9.ktiles = s32[8,4]{1,0:T(8,128)} copy(s32[8,4]{0,1:T(4,128)} %param.10) | data formatting | bytes 256 | tf_op args[2]
  1.3 1.3 %copy.10.htiles = s32[8,4]{1,0:T(8,128)} copy(s32[8,4]{0,1:T(4,128)} %param.11) | data formatting | bytes 256 | tf_op args[3]
  2.7 32.7 %shard_map.82 = f32[1,64,512]{2,1,0:T(8,128)} custom-call(s32[8,4]{1,0:T(8,128)} %copy.9.ktiles, s32[8,4]{1,0:T(8,128)} %copy.10.htiles, s32[64]{0:T(128)} %rows.1, s32[64]{0:T(128)} %cols.1, s32[1,4]{1,0:T(1,128)} %owner.1, bf16[512,256]{1,0:T(8,128)(2,1)} %k_hbm.1, bf16[512,256]{1,0:T(8,128)(2,1)} %h_hbm.1, bf16[4096,512]{1,0:T(8,128)(2,1)} %bitcast.1), custom_call_target="tpu_custom_call" | custom-call | tf_op jit(solution)/shard_map/pallas_call | solution.py:273
  35.4 1.6 %copy.12 = f32[1,64,512]{2,1,0:T(8,128)} copy(f32[1,64,512]{2,1,0:T(8,128)} %shard_map.82) | data formatting | bytes 262144

commit v2 on v1

--- a/solution.py
+++ b/solution.py
@@ -30,7 +30,7 @@
     n = lax.axis_index("narrow")
     chips = n_narrow // 2
     chip, core = n // 2, n % 2
-    tile_rows, tile_cols = htiles.shape
+    tile_cols, tile_rows = htiles.shape
     height, kcols = k_hbm.shape
     hrows, breadth = h_hbm.shape
     per = hrows // kcols
@@ -61,7 +61,7 @@
         lane_tile = lax.broadcasted_iota(jnp.int32, (1, extent), 1) // tile
         mask = jnp.zeros((1, extent), jnp.float32)
         for a in range(tile_cols):
-            mask = jnp.where(lane_tile == a, tiles[b, a].astype(jnp.float32), mask)
+            mask = jnp.where(lane_tile == a, tiles[a, b].astype(jnp.float32), mask)
         return mask.astype(jnp.bfloat16)
 
     load_h.wait()
@@ -73,11 +73,6 @@
         col = lax.broadcasted_iota(jnp.int32, (width, breadth), 1)
         pick = (col == (r // jc) * tile + c * jc + r % jc).astype(jnp.float32).astype(jnp.bfloat16)
         hbuf[c, z] = lax.dot_general(pick, h_in[...], NT, preferred_element_type=jnp.float32).astype(jnp.bfloat16)
-    load_k.wait()
-    for b in range(tile_rows):
-        span = pl.ds(b * tile, tile)
-        kbuf[n, span, :] = k_in[span, :] * mask_rows(ktiles, b, kcols)
-
     pl.semaphore_wait(barrier, chips - 1 + 1 + n_wide - 1)
 
     def unit(u, src):
@@ -142,6 +137,10 @@
 
     h_own(0)
     h_own(1)
+    load_k.wait()
+    for b in range(tile_rows):
+        span = pl.ds(b * tile, tile)
+        kbuf[n, span, :] = k_in[span, :] * mask_rows(ktiles, b, kcols)
     for g in range(1, chips):
         k_copy(g).start()
     sib_copy(0, core).start()
@@ -268,7 +267,7 @@
     width, jc = breadth // CHUNKS, tile // CHUNKS
     chips = n_narrow // 2
     smem = pl.BlockSpec(memory_space=pltpu.SMEM)
-    hbm = pl.BlockSpec(memory_space=pl.ANY)
+    hbm = pl.BlockSpec(memory_space=pltpu.HBM)
     dma = pltpu.SemaphoreType.DMA
     return pl.pallas_call(
         functools.partial(kernel_body, n_wide, n_narrow, tile),
@@ -295,7 +294,7 @@
         ],
         compiler_params=pltpu.CompilerParams(
             collective_id=0, has_side_effects=True, vmem_limit_bytes=60 * 2**20),
-    )(kernel_tiles, ham_tiles, pair_row, pair_col, owner, kernel, hamiltonian,
+    )(kernel_tiles.T, ham_tiles.T, pair_row, pair_col, owner, kernel, hamiltonian,
       sphere_phi.reshape(pairs * tile, pts))
 
 

time: 37.2 us -> 34.4 us (0.925)
  local copies, waits for them, and re-layouts: 4.26 us -> 1.57 us
    unnamed x3 -> x1, local copies, waits for them, and re-layouts: 4.26 us -> 1.57 us
where the time goes in v2:
time: 34.4 us; the launch traced here: 34.2 us
  Pallas kernels  32.6 us (95%)
  local copies, waits for them, and re-layouts  1.57 us (5%)
    pallas_call x1, Pallas kernels, body(): pl.pallas_call(functools.partial(kernel_body, n_wide, n_narrow, tile), ou...  32.6 us
    unnamed x1, local copies, waits for them, and re-layouts  1.57 us

profile of v2, /device:TPU:0, one launch (start us, length us, event | category | flops | bytes accessed | tf_op | source)
XLA Modules:
  0.0 34.2 jit_solution(4587559067402605998)
XLA Ops:
  0.0 32.6 %shard_map.82 = f32[1,64,512]{2,1,0:T(8,128)} custom-call(s32[4,8]{1,0:T(4,128)} %bitcast.4, s32[4,8]{1,0:T(4,128)} %bitcast.5, s32[64]{0:T(128)} %rows.1, s32[64]{0:T(128)} %cols.1, s32[1,4]{1,0:T(1,128)} %owner.1, bf16[512,256]{1,0:T(8,128)(2,1)} %k_hbm.1, bf16[512,256]{1,0:T(8,128)(2,1)} %h_hbm.1, bf16[4096,512]{1,0:T(8,128)(2,1)} %bitcast.3), custom_call_target="tpu_custom_call" | custom-call | tf_op jit(solution)/shard_map/pallas_call | solution.py:272
  32.7 1.6 %copy.10 = f32[1,64,512]{2,1,0:T(8,128)} copy(f32[1,64,512]{2,1,0:T(8,128)} %shard_map.82) | data formatting | bytes 262144

commit v3 on v2

--- a/solution.py
+++ b/solution.py
@@ -22,8 +22,8 @@
 
 def kernel_body(
     n_wide, n_narrow, tile,
-    ktiles, htiles, rows, cols, owner, k_hbm, h_hbm, phi_hbm, out_ref,
-    k_in, h_in, phi, kbuf, hbuf, acc, table, lhs, own, stage, landed,
+    ktiles_hbm, htiles_hbm, rows_hbm, cols_hbm, owner_hbm, k_hbm, h_hbm, phi_hbm, out_ref,
+    ktiles, htiles, rows, cols, owner, k_in, h_in, phi, kbuf, hbuf, acc, table, lhs, own, stage, landed,
     in_sem, k_send, k_recv, s_send, s_recv, h_send, h_recv, r_send, r_recv,
 ):
     z = lax.axis_index("wide")
@@ -53,8 +53,16 @@
     load_h = pltpu.make_async_copy(h_hbm, h_in, in_sem.at[0])
     load_k = pltpu.make_async_copy(k_hbm, k_in, in_sem.at[1])
     load_p = pltpu.make_async_copy(phi_hbm, phi, in_sem.at[2])
+    tables = [
+        pltpu.make_async_copy(a, b, in_sem.at[3 + i])
+        for i, (a, b) in enumerate((
+            (htiles_hbm, htiles), (ktiles_hbm, ktiles), (rows_hbm, rows), (cols_hbm, cols), (owner_hbm, owner)))
+    ]
+    tables[0].start()
     load_h.start()
     load_k.start()
+    for load in tables[1:]:
+        load.start()
     load_p.start()
 
     def mask_rows(tiles, b, extent):
@@ -64,6 +72,7 @@
             mask = jnp.where(lane_tile == a, tiles[a, b].astype(jnp.float32), mask)
         return mask.astype(jnp.bfloat16)
 
+    tables[0].wait()
     load_h.wait()
     for b in range(tile_rows):
         span = pl.ds(b * tile, tile)
@@ -137,6 +146,7 @@
 
     h_own(0)
     h_own(1)
+    tables[1].wait()
     load_k.wait()
     for b in range(tile_rows):
         span = pl.ds(b * tile, tile)
@@ -145,20 +155,21 @@
         k_copy(g).start()
     sib_copy(0, core).start()
 
+    h_own(2)
     h_arrive(0, 1)
-    h_own(2)
+    h_arrive(1, 1)
+    h_arrive(2, 1)
     for s in range(2, n_wide - 1):
         h_arrive(0, s)
     for g in range(1, chips - 1):
         k_arrived(g)
         sib_copy(g, core).start()
-    h_arrive(1, 1)
-    h_arrive(2, 1)
+    for s in range(2, n_wide - 1):
+        h_arrive(1, s)
     k_arrived(chips - 1)
     sib_copy(chips - 1, core).start()
     h_arrive(0, n_wide - 1)
     for s in range(2, n_wide - 1):
-        h_arrive(1, s)
         h_arrive(2, s)
     for g in range(chips):
         sib_copy(g, 1 - core).wait_recv()
@@ -217,6 +228,8 @@
         lax.fori_loop(lo, hi, step, 0)
 
     load_p.wait()
+    for load in tables[2:]:
+        load.wait()
     loop(0, 0, n_wide)
     finish(0)
     for s in range(1, n_wide):
@@ -266,15 +279,19 @@
     tile_rows, tile_cols = ham_tiles.shape
     width, jc = breadth // CHUNKS, tile // CHUNKS
     chips = n_narrow // 2
-    smem = pl.BlockSpec(memory_space=pltpu.SMEM)
     hbm = pl.BlockSpec(memory_space=pltpu.HBM)
     dma = pltpu.SemaphoreType.DMA
     return pl.pallas_call(
         functools.partial(kernel_body, n_wide, n_narrow, tile),
         out_shape=jax.ShapeDtypeStruct((1, tile, pts), jnp.float32),
-        in_specs=[smem] * 5 + [hbm] * 3,
+        in_specs=[hbm] * 8,
         out_specs=pl.BlockSpec(memory_space=pltpu.VMEM),
         scratch_shapes=[
+            pltpu.SMEM((tile_cols, tile_rows), jnp.int32),
+            pltpu.SMEM((tile_cols, tile_rows), jnp.int32),
+            pltpu.SMEM((pairs,), jnp.int32),
+            pltpu.SMEM((pairs,), jnp.int32),
+            pltpu.SMEM((1, tile_cols), jnp.int32),
             pltpu.VMEM((height, kcols), jnp.bfloat16),
             pltpu.VMEM((hrows, breadth), jnp.bfloat16),
             pltpu.VMEM((pairs * tile, pts), jnp.bfloat16),
@@ -286,7 +303,7 @@
             pltpu.VMEM((CHUNKS, n_wide, jc, pts), jnp.float32),
             pltpu.VMEM((CHUNKS, n_wide, jc, pts), jnp.bfloat16),
             pltpu.VMEM((CHUNKS, n_wide - 1, jc, pts), jnp.bfloat16),
-            dma((3,)),
+            dma((8,)),
             dma((chips,)), dma((chips,)),
             dma((chips,)), dma((chips,)),
             dma((3, 2, n_wide)), dma((3, 2, n_wide)),

time: 34.4 us -> 33.5 us (0.974)
  Pallas kernels: 32.6 us -> 31.7 us
    pallas_call x1, Pallas kernels: 32.6 us -> 31.7 us  [body(): pl.pallas_call(functools.partial(kernel_body, n_wide, n_narrow, tile), ou...]
where the time goes in v3:
time: 33.5 us; the launch traced here: 33.3 us
  Pallas kernels  31.7 us (95%)
  local copies, waits for them, and re-layouts  1.57 us (5%)
    pallas_call x1, Pallas kernels, body(): pl.pallas_call(functools.partial(kernel_body, n_wide, n_narrow, tile), ou...  31.7 us
    unnamed x1, local copies, waits for them, and re-layouts  1.57 us

profile of v3, /device:TPU:0, one launch (start us, length us, event | category | flops | bytes accessed | tf_op | source)
XLA Modules:
  0.0 33.3 jit_solution(15715361503887948091)
XLA Ops:
  0.0 31.7 %shard_map.82 = f32[1,64,512]{2,1,0:T(8,128)} custom-call(s32[4,8]{1,0:T(4,128)} %bitcast.4, s32[4,8]{1,0:T(4,128)} %bitcast.5, s32[64]{0:T(128)} %rows_hbm.1, s32[64]{0:T(128)} %cols_hbm.1, s32[1,4]{1,0:T(1,128)} %owner_hbm.1, bf16[512,256]{1,0:T(8,128)(2,1)} %k_hbm.1, bf16[512,256]{1,0:T(8,128)(2,1)} %h_hbm.1, bf16[4096,512]{1,0:T(8,128)(2,1)} %bitcast.3), custom_call_target="tpu_custom_call" | custom-call | tf_op jit(solution)/shard_map/pallas_call | solution.py:284
  31.7 1.6 %copy.10 = f32[1,64,512]{2,1,0:T(8,128)} copy(f32[1,64,512]{2,1,0:T(8,128)} %shard_map.82) | data formatting | bytes 262144
